TPU v7x, 32 devices: a whole 2x2x4 slice. The times are simulated.
32 devices in a mesh: grp: 2 (over x), seq: 8 (over z, y), head: 2 (over core).
Axes of the slice: x: 2, y: 2, z: 4, core: 2. Of those that a mesh axis runs over, the one named last changes fastest.
Arguments:
- q_nope: bfloat16 [8, 128, 128], P('grp', ('seq', 'head')), parts along dimension 0, may hold values from -6 to 6
- q_rope: bfloat16 [8, 128, 64], P('grp', ('seq', 'head')), parts along dimension 0, may hold values from -150 to 150
- w_uk: bfloat16 [128, 128, 512], P(('seq', 'head')), may hold values from -0.5 to 0.5
- w_uv: bfloat16 [128, 512, 128], P(('seq', 'head')), may hold values from -1 to 1
- cache: bfloat16 [8, 4096, 576], P('grp', 'seq'), parts along dimension 0, may hold values from -12 to 12
- lengths: int32 [8], P('grp'), parts along dimension 0, may hold values from 2048 to 4096, as said below
- selected: int32 [8, 8, 32], P('grp'), parts along dimension 0, may hold values from 0 to 63, as said below
Outputs:
- attended: bfloat16 [8, 128, 128], P('grp', ('seq', 'head')), parts along dimension 0
- bounds: float32 [8, 8, 64], P('grp', None, 'seq'), parts along dimension 0
There are 2 independent parts, one for each index of `grp`. A program takes and returns all parts, laid end to end along the dimension named above; an argument that names none is the same for every part. Nothing has to cross between parts.
Inputs may be any that keep to these rules, and one draw needn't show every extreme that they name: `lengths`: some request has exactly 4096 cached tokens; every request has 2048 or more. `selected`: for each request and head group the 32 page numbers are distinct and below ceil(lengths[r] / 64); page 0 and the page of the request's last cached token are always among them.
All inputs are finite; a program needn't handle non-finite values.
Results may differ from a plain program's by a relative error of at most 0.0065.
Values may be sent and summed in bfloat16 or wider, within the bound.
A program may use at most 64 MiB of HBM per device.

v0:
```python
import jax
import jax.numpy as jnp
from jax import lax
from jax.sharding import PartitionSpec as P

GH = 16
PAGE = 64


def local(q_nope, q_rope, w_uk, w_uv, cache, lengths, selected):
    seq_count = lax.axis_size("seq")
    head_count = lax.axis_size("head")
    seq_rank = lax.axis_index("seq")
    head_rank = lax.axis_index("head")
    requests = q_nope.shape[0]
    head_block = q_nope.shape[1]
    latent_width = w_uk.shape[2]
    cache_width = cache.shape[2]
    tokens_here = cache.shape[1]
    pages_here = tokens_here // PAGE
    groups = selected.shape[1]
    softmax_scale = (q_nope.shape[2] + q_rope.shape[2]) ** (-0.5)
    query_latent = jnp.einsum(
        "rhn,hnl->rhl", q_nope, w_uk, preferred_element_type=jnp.float32
    ).astype(jnp.bfloat16)
    absorbed = jnp.concatenate([query_latent, q_rope], axis=2)
    queries = lax.all_gather(absorbed, "seq", axis=1, tiled=True)
    heads_here = head_block * seq_count
    position = jnp.arange(heads_here, dtype=jnp.int32)
    global_head = (
        position // head_block * head_count + head_rank
    ) * head_block + position % head_block
    group_of = global_head // GH
    group_hot = group_of[:, None] == jnp.arange(groups, dtype=jnp.int32)[None, :]
    page_number = seq_rank * pages_here + jnp.arange(pages_here, dtype=jnp.int32)
    token_index = seq_rank * tokens_here + jnp.arange(tokens_here, dtype=jnp.int32).reshape(
        pages_here, PAGE
    )
    live_token = token_index[None] < lengths[:, None, None]
    live_page = live_token[:, :, 0]
    page_blocks = cache.reshape(requests, pages_here, PAGE, cache_width)
    page_low = jnp.min(jnp.where(live_token[..., None], page_blocks, jnp.inf), axis=2).astype(
        jnp.float32
    )
    page_high = jnp.max(jnp.where(live_token[..., None], page_blocks, -jnp.inf), axis=2).astype(
        jnp.float32
    )
    page_low = jnp.where(live_page[..., None], page_low, 0.0)
    page_high = jnp.where(live_page[..., None], page_high, 0.0)
    middle = (page_low + page_high) * 0.5
    spread = (page_high - page_low) * 0.5
    query_float = queries.astype(jnp.float32)
    head_bound = softmax_scale * (
        jnp.einsum("rhd,rpd->rhp", query_float, middle, precision=lax.Precision.HIGHEST)
        + jnp.einsum("rhd,rpd->rhp", jnp.abs(query_float), spread, precision=lax.Precision.HIGHEST)
    )
    group_bound = jnp.max(
        jnp.where(group_hot.T[None, :, :, None], head_bound[:, None, :, :], -1e30), axis=2
    )
    group_bound = lax.pmax(group_bound, "head")
    bounds = jnp.where(live_page[:, None, :], group_bound, 0.0)
    picked = jnp.any(selected[:, :, :, None] == page_number[None, None, None, :], axis=2)
    head_pick = jnp.any(group_hot[None, :, :, None] & picked[:, None, :, :], axis=2)
    scores = (
        jnp.einsum("rhd,rtd->rht", queries, cache, preferred_element_type=jnp.float32)
        * softmax_scale
    )
    scores = scores.reshape(requests, heads_here, pages_here, PAGE)
    scores = jnp.where(live_token[:, None], scores, -1e30)
    page_top = jnp.max(scores, axis=3)
    weights = jnp.where(live_token[:, None], jnp.exp(scores - page_top[..., None]), 0.0).astype(
        jnp.bfloat16
    )
    page_total = jnp.sum(weights.astype(jnp.float32), axis=3)
    page_weighted = jnp.einsum(
        "rhpt,rptl->rhpl",
        weights,
        page_blocks[..., :latent_width],
        preferred_element_type=jnp.float32,
    )
    summit = jnp.max(jnp.where(head_pick, page_top, -1e30), axis=2)
    factor = jnp.where(head_pick, jnp.exp(page_top - summit[..., None]), 0.0)
    total = jnp.sum(factor * page_total, axis=2)
    weighted = jnp.einsum("rhp,rhpl->rhl", factor, page_weighted, precision=lax.Precision.HIGHEST)
    gotten = (
        lax.all_to_all(
            summit.reshape(requests, seq_count, head_block),
            "seq",
            split_axis=1,
            concat_axis=1,
            tiled=True,
        ),
        lax.all_to_all(
            total.reshape(requests, seq_count, head_block),
            "seq",
            split_axis=1,
            concat_axis=1,
            tiled=True,
        ),
        lax.all_to_all(
            weighted.reshape(requests, seq_count, head_block, latent_width),
            "seq",
            split_axis=1,
            concat_axis=1,
            tiled=True,
        ),
    )
    highest = jnp.max(gotten[0], axis=1)
    rescale = jnp.exp(gotten[0] - highest[:, None, :])
    own_total = jnp.sum(rescale * gotten[1], axis=1)
    own_weighted = jnp.sum(rescale[..., None] * gotten[2], axis=1)
    latent_out = (own_weighted / own_total[..., None]).astype(jnp.bfloat16)
    attended = jnp.einsum(
        "rhl,hlv->rhv", latent_out, w_uv, preferred_element_type=jnp.float32
    ).astype(jnp.bfloat16)
    return (attended, bounds)


def solution(mesh):
    placed = (
        P("grp", ("seq", "head"), None),
        P("grp", ("seq", "head"), None),
        P(("seq", "head"), None, None),
        P(("seq", "head"), None, None),
        P("grp", "seq", None),
        P("grp"),
        P("grp", None, None),
    )
    return jax.shard_map(
        local,
        mesh=mesh,
        in_specs=placed,
        out_specs=(P("grp", ("seq", "head"), None), P("grp", None, "seq")),
        check_vma=False,
    )
```

profile of v0, /device:TPU:0, one launch (start us, length us, event | category | flops | bytes accessed | tf_op | source)
XLA Modules:
  0.0 88.1 jit_solution(16813406923026156517)
XLA Ops:
  0.7 0.8 copy.102
  1.5 0.4 copy-done
  1.9 0.9 %fusion.3 = bf16[4,8,512]{2,0,1:T(4,128)(2,1)S(1)} fusion(bf16[8,128,512]{2,1,0:T(8,128)(2,1)S(1)} %copy-done, bf16[4,8,128]{2,1,0:T(8,128)(2,1)} %param.7), kind=kOutput, calls=%fused_computation.8 | convolution fusion | flops 4210688 | bytes 1089536 | tf_op jit(solution)/shard_map/rhn,hnl->rhl/dot_general | solution.py:23
  2.9 32.7 %all_gather.3 = bf16[4,64,576]{2,0,1:T(4,128)(2,1)S(1)} all-gather(bf16[4,8,576]{2,0,1:T(4,128)(2,1)S(1)} %pad_maximum_fusion), channel_id=1, replica_groups=mesh['grp'=2,'seq'=8,'head'=2] {'seq'}, dimensions={1}, use_global_device_ids=true | all-gather | bytes 331776 | tf_op jit(solution)/shard_map/all_gather | solution.py:27
  35.5 2.2 %convolution_multiply_fusion = f32[4,64,512]{2,1,0:T(8,128)S(1)} fusion(bf16[4,512,576]{1,2,0:T(8,128)(2,1)} %param.11, bf16[4,64,576]{2,0,1:T(4,128)(2,1)S(1)} %all_gather.3), kind=kOutput, calls=%fused_computation.6 | convolution fusion | flops 151126016 | bytes 3178496 | tf_op jit(solution)/shard_map/rhd,rtd->rht/dot_general | solution.py:65
  38.0 0.7 compare_reduce_fusion
  39.3 0.6 copy.105
  39.9 5.6 %all-to-all-start = ((f32[4,8,8]{2,0,1:T(4,128)}), f32[4,8,8]{2,0,1:T(4,128)S(1)}, u32[]{:S(2)}, u32[]{:S(2)}) async-start(f32[4,8,8]{2,0,1:T(4,128)} %copy.105), calls=%async_computation | async-start | bytes 32768 | tf_op jit(solution)/shard_map/all_to_all | solution.py:86
  45.5 0.7 convert_reduce_fusion
  46.2 4.3 %copy.106 = bf16[4,512,576]{2,1,0:T(8,128)(2,1)} copy(bf16[4,512,576]{1,2,0:T(8,128)(2,1)} %param.11) | data formatting | bytes 4718592 | tf_op args[4]
  50.7 2.7 %select_reduce_fusion.1 = (bf16[4,8,576]{2,1,0:T(8,128)(2,1)S(1)}, bf16[4,8,576]{2,1,0:T(8,128)(2,1)S(1)}) fusion(pred[4,8,64]{2,1,0:T(8,128)(4,1)S(1)} %broadcast_compare_fusion, bf16[4,512,576]{2,1,0:T(8,128)(2,1)} %copy.106), kind=kLoop, calls=%fused_computation.3 | loop fusion | flops 4681728 | bytes 2435072 | tf_op jit(solution)/shard_map/reduce_min | solution.py:42
  53.4 1.0 %convolution_bitcast_fusion = f32[4,64,8,512]{3,1,2,0:T(8,128)S(1)} fusion(bf16[4,8,64,576]{3,2,1,0:T(8,128)(2,1)S(1)} %bitcast.20, f32[4,64,8,64]{3,2,1,0:T(8,128)S(1)} %reshape.136, f32[4,64,8]{1,2,0:T(8,128)S(1)} %fusion.6, pred[4,8,64]{2,1,0:T(8,128)(4,1)S(1)} %broadcast_compare_fusion), kind=kOutput, calls=%fused_computation.4 | convolution fusion | flops 134742016 | bytes 7360512 | tf_op jit(solution)/shard_map/rhpt,rptl->rhpl/dot_general | solution.py:75
  54.4 5.4 %fusion = f32[4,64,1,512]{3,2,1,0:T(1,128)S(1)} fusion(f32[4,64,8,1]{2,3,1,0:T(1,128)S(1)} %copy.114, f32[4,64,8,512]{3,1,2,0:T(8,128)S(1)} %convolution_bitcast_fusion), kind=kOutput, calls=%fused_computation | convolution fusion | flops 12582912 | bytes 4726784 | tf_op jit(solution)/shard_map/rhp,rhpl->rhl/dot_general | solution.py:84
  60.0 0.6 copy.108
  60.7 6.0 %all-to-all-start.2 = ((f32[4,8,8]{2,0,1:T(4,128)}), f32[4,8,8]{2,0,1:T(4,128)S(1)}, u32[]{:S(2)}, u32[]{:S(2)}) async-start(f32[4,8,8]{2,0,1:T(4,128)} %copy.108), calls=%async_computation.2 | async-start | bytes 32768 | tf_op jit(solution)/shard_map/all_to_all | solution.py:93
  66.7 0.5 fusion.10
  67.2 0.8 copy.107
  68.0 5.3 %all-to-all-done.2 = f32[4,8,8]{2,0,1:T(4,128)S(1)} async-done(((f32[4,8,8]{2,0,1:T(4,128)}), f32[4,8,8]{2,0,1:T(4,128)S(1)}, u32[]{:S(2)}, u32[]{:S(2)}) %all-to-all-start.2) | async-done | bytes 1056 | tf_op jit(solution)/shard_map/all_to_all | solution.py:93
  73.3 3.5 %all-to-all-start.1 = ((f32[4,8,8,512]{3,2,0,1:T(8,128)}), f32[4,8,8,512]{3,2,0,1:T(8,128)S(1)}, u32[]{:S(2)}, u32[]{:S(2)}) async-start(f32[4,8,8,512]{3,2,0,1:T(8,128)} %copy.107), calls=%async_computation.1 | async-start | bytes 1048576 | tf_op jit(solution)/shard_map/all_to_all | solution.py:100
  76.8 0.8 fusion.4
  77.7 3.4 %pmax.7 = f32[4,8,8]{2,1,0:T(8,128)S(1)} all-reduce(f32[4,8,8]{2,1,0:T(8,128)S(1)} %select_reduce_fusion.2), channel_id=1, replica_groups=mesh['grp'=2,'seq'=8,'head'=2] {'head'}, use_global_device_ids=true, to_apply=%region_12.13 | all-reduce | flops 256 | bytes 2048 | tf_op jit(solution)/shard_map/pmax | solution.py:60
  81.1 0.6 broadcast_select_fusion
  81.8 5.2 %all-to-all-done.1 = f32[4,8,8,512]{3,2,0,1:T(8,128)S(1)} async-done(((f32[4,8,8,512]{3,2,0,1:T(8,128)}), f32[4,8,8,512]{3,2,0,1:T(8,128)S(1)}, u32[]{:S(2)}, u32[]{:S(2)}) %all-to-all-start.1) | async-done | bytes 524320 | tf_op jit(solution)/shard_map/all_to_all | solution.py:100
  87.4 0.6 copy.113
  (33 shorter events, 1.9 us)
Async XLA Ops:
  0.6 1.2 %copy-start = (bf16[8,128,512]{2,1,0:T(8,128)(2,1)S(1)}, bf16[8,128,512]{2,1,0:T(8,128)(2,1)}, u32[]{:S(2)}) copy-start(bf16[8,128,512]{2,1,0:T(8,128)(2,1)} %param.9) | copy-start | bytes 3145732
  2.8 35.1 %copy-start.3 = (s32[4,8,32]{2,1,0:T(8,128)S(1)}, s32[4,8,32]{2,1,0:T(8,128)}, u32[]{:S(2)}) copy-start(s32[4,8,32]{2,1,0:T(8,128)} %param.13) | copy-start | bytes 12292
  2.8 36.0 %copy-start.4 = (s32[4]{0:T(128)S(1)}, s32[4]{0:T(128)}, u32[]{:S(2)}) copy-start(s32[4]{0:T(128)} %param.12) | copy-start | bytes 52
  39.9 20.7 %all-to-all-start = ((f32[4,8,8]{2,0,1:T(4,128)}), f32[4,8,8]{2,0,1:T(4,128)S(1)}, u32[]{:S(2)}, u32[]{:S(2)}) async-start(f32[4,8,8]{2,0,1:T(4,128)} %copy.105), calls=%async_computation | async-start | bytes 32768 | tf_op jit(solution)/shard_map/all_to_all | solution.py:86
  50.7 2.7 %copy-start.1 = (bf16[4,512,576]{2,1,0:T(8,128)(2,1)S(1)}, bf16[4,512,576]{2,1,0:T(8,128)(2,1)}, u32[]{:S(2)}) copy-start(bf16[4,512,576]{2,1,0:T(8,128)(2,1)} %copy.106) | copy-start | bytes 7077892
  60.7 12.6 %all-to-all-start.2 = ((f32[4,8,8]{2,0,1:T(4,128)}), f32[4,8,8]{2,0,1:T(4,128)S(1)}, u32[]{:S(2)}, u32[]{:S(2)}) async-start(f32[4,8,8]{2,0,1:T(4,128)} %copy.108), calls=%async_computation.2 | async-start | bytes 32768 | tf_op jit(solution)/shard_map/all_to_all | solution.py:93
  66.7 20.5 %copy-start.2 = (bf16[8,512,128]{2,1,0:T(8,128)(2,1)S(1)}, bf16[8,512,128]{2,1,0:T(8,128)(2,1)}, u32[]{:S(2)}) copy-start(bf16[8,512,128]{2,1,0:T(8,128)(2,1)} %param.10) | copy-start | bytes 3145732
  73.3 13.7 %all-to-all-start.1 = ((f32[4,8,8,512]{3,2,0,1:T(8,128)}), f32[4,8,8,512]{3,2,0,1:T(8,128)S(1)}, u32[]{:S(2)}, u32[]{:S(2)}) async-start(f32[4,8,8,512]{3,2,0,1:T(8,128)} %copy.107), calls=%async_computation.1 | async-start | bytes 1048576 | tf_op jit(solution)/shard_map/all_to_all | solution.py:100
where the time goes:
time: 88.6 us; the launch traced here: 88.1 us
  blocking collectives  36 us (41%)
  starting transfers between devices  15.1 us (17%)
  matrix products  11 us (12%)
  waiting for transfers between devices  10.5 us (12%)
  local copies, waits for them, and re-layouts  8.85 us (10%)
  other arithmetic  5.68 us (6%)
    all_gather x1, blocking collectives, local(): queries = lax.all_gather(absorbed, 'seq', axis=1, tiled=True)  32.7 us
    unnamed x13, local copies, waits for them, and re-layouts  6.15 us
    all_to_all x1, starting transfers between devices, local(): lax.all_to_all(total.reshape(requests, seq_count, head_block), 'seq', spl...  6.01 us
    all_to_all x1, starting transfers between devices, local(): lax.all_to_all(summit.reshape(requests, seq_count, head_block), 'seq', sp...  5.61 us
    dot_general x1, matrix products, local(): jnp.einsum('rhp,rhpl->rhl', factor, page_weighted, precision=lax.Precisio...  5.37 us
    all_to_all x1, waiting for transfers between devices, local(): lax.all_to_all(total.reshape(requests, seq_count, head_block), 'seq', spl...  5.28 us
    all_to_all x1, waiting for transfers between devices, local(): lax.all_to_all(weighted.reshape(requests, seq_count, head_block, latent_w...  5.23 us
    all_to_all x1, starting transfers between devices, local(): lax.all_to_all(weighted.reshape(requests, seq_count, head_block, latent_w...  3.49 us
  transfers between devices with their start and end apart: 3, of which 2 were waited for; matrix products, arithmetic and copies ran while one was open for 20% of the time, Pallas kernels for 0%

commit v1 on v0

--- a/solution.py
+++ b/solution.py
@@ -24,7 +24,14 @@
         "rhn,hnl->rhl", q_nope, w_uk, preferred_element_type=jnp.float32
     ).astype(jnp.bfloat16)
     absorbed = jnp.concatenate([query_latent, q_rope], axis=2)
-    queries = lax.all_gather(absorbed, "seq", axis=1, tiled=True)
+    x = absorbed
+    ways, here, lap = (lax.axis_size("seq"), lax.axis_index("seq"), x.shape[1])
+    dims = [n * ways if d == 1 else n for d, n in enumerate(x.shape)]
+    full = lax.dynamic_update_slice_in_dim(jnp.zeros(dims, x.dtype), x, here * lap, axis=1)
+    for far in range(1, ways):
+        x = lax.ppermute(x, "seq", [(d, (d + 1) % ways) for d in range(ways)])
+        full = lax.dynamic_update_slice_in_dim(full, x, (here - far) % ways * lap, axis=1)
+    queries = full
     heads_here = head_block * seq_count
     position = jnp.arange(heads_here, dtype=jnp.int32)
     global_head = (

time: 88.6 us -> 105 us (1.19)
  blocking collectives: 36 us -> 3.36 us
  waiting for transfers between devices: 10.5 us -> 39.3 us
  matrix products: 11 us -> 19.2 us
  local copies, waits for them, and re-layouts: 8.85 us -> 15.7 us
  starting transfers between devices: 15.1 us -> 18.5 us
  other arithmetic: 5.68 us -> 7.2 us
    ppermute x0 -> x7, waiting for transfers between devices: none -> 34.9 us  [local(): x = lax.ppermute(x, 'seq', [(d, (d + 1) % ways) for d in range(ways)])]
    all_gather x1 -> x0, blocking collectives: 32.7 us -> none  [local(): queries = lax.all_gather(absorbed, 'seq', axis=1, tiled=True)]
    dynamic_update_slice x0 -> x8, local copies, waits for them, and re-layouts: none -> 5.02 us  [the longest x7 4.4 us: local(): lax.dynamic_update_slice_in_dim(full, x, (here - far) % ways * lap, axis=1)]
    ppermute x0 -> x7, starting transfers between devices: none -> 4.63 us  [local(): x = lax.ppermute(x, 'seq', [(d, (d + 1) % ways) for d in range(ways)])]
    all_to_all x1, waiting for transfers between devices: 5.28 us -> 1.46 us  [local(): lax.all_to_all(total.reshape(requests, seq_count, head_block), 'seq', spl...]
    dot_general x1, matrix products: 1.03 us -> 4.28 us  [local(): jnp.einsum('rhpt,rptl->rhpl', weights, page_blocks[..., :latent_width], p...]
    dot_general x1, matrix products: 5.37 us -> 8.21 us  [local(): jnp.einsum('rhp,rhpl->rhl', factor, page_weighted, precision=lax.Precisio...]
    all_to_all x1, starting transfers between devices: 6.01 us -> 3.34 us  [local(): lax.all_to_all(total.reshape(requests, seq_count, head_block), 'seq', spl...]
  transfers between devices with their start and end apart: 3 -> 10, of which waited for: 2 -> 8; matrix products, arithmetic and copies ran while one was open for 20% -> 32% of each run, Pallas kernels for 0% -> 0%
where the time goes in v1:
time: 105 us; the launch traced here: 104 us
  waiting for transfers between devices  39.3 us (37%)
  matrix products  19.2 us (18%)
  starting transfers between devices  18.5 us (18%)
  local copies, waits for them, and re-layouts  15.7 us (15%)
  other arithmetic  7.2 us (7%)
  blocking collectives  3.36 us (3%)
    ppermute x7, waiting for transfers between devices, local(): x = lax.ppermute(x, 'seq', [(d, (d + 1) % ways) for d in range(ways)])  34.9 us
    dot_general x1, matrix products, local(): jnp.einsum('rhp,rhpl->rhl', factor, page_weighted, precision=lax.Precisio...  8.21 us
    unnamed x19, local copies, waits for them, and re-layouts  6.25 us
    all_to_all x1, starting transfers between devices, local(): lax.all_to_all(weighted.reshape(requests, seq_count, head_block, latent_w...  6 us
    ppermute x7, starting transfers between devices, local(): x = lax.ppermute(x, 'seq', [(d, (d + 1) % ways) for d in range(ways)])  4.63 us
    all_to_all x1, starting transfers between devices, local(): lax.all_to_all(summit.reshape(requests, seq_count, head_block), 'seq', sp...  4.52 us
    dynamic_update_slice x7, local copies, waits for them, and re-layouts, local(): lax.dynamic_update_slice_in_dim(full, x, (here - far) % ways * lap, axis=1)  4.4 us
    dot_general x1, matrix products, local(): jnp.einsum('rhpt,rptl->rhpl', weights, page_blocks[..., :latent_width], p...  4.28 us
  transfers between devices with their start and end apart: 10, of which 8 were waited for; matrix products, arithmetic and copies ran while one was open for 32% of the time, Pallas kernels for 0%

profile of v1, /device:TPU:0, one launch (start us, length us, event | category | flops | bytes accessed | tf_op | source)
XLA Modules:
  0.0 104.2 jit_solution(5016037063882922585)
XLA Ops:
  1.9 0.9 fusion.3
  2.9 3.0 %collective-permute-start = (bf16[4,8,576]{2,0,1:T(4,128)(2,1)S(1)}, bf16[4,8,576]{2,0,1:T(4,128)(2,1)S(1)}, u32[]{:S(2)}, u32[]{:S(2)}) collective-permute-start(bf16[4,8,576]{2,0,1:T(4,128)(2,1)S(1)} %pad_maximum_fusion), channel_id=1, source_target_pairs={{0,2},{2,4},{4,6},{6,8},{8,10},{10,12},{12,14},{14,0},{1,3},{3,5},... | collective-permute-start | bytes 110600 | tf_op jit(solution)/shard_map/ppermute | solution.py:32
  7.0 4.4 %copy.148 = bf16[4,512,576]{2,1,0:T(8,128)(2,1)} copy(bf16[4,512,576]{1,2,0:T(8,128)(2,1)} %param.11) | data formatting | bytes 4718592 | tf_op args[4]
  12.9 3.1 %select_reduce_fusion.1 = (bf16[4,8,576]{2,1,0:T(8,128)(2,1)S(1)}, bf16[4,8,576]{2,1,0:T(8,128)(2,1)}) fusion(pred[4,8,64]{2,1,0:T(8,128)(4,1)S(1)} %broadcast_compare_fusion, bf16[4,512,576]{2,1,0:T(8,128)(2,1)} %copy.148), kind=kLoop, calls=%fused_computation.3 | loop fusion | flops 4681728 | bytes 2435072 | tf_op jit(solution)/shard_map/reduce_min | solution.py:49
  17.1 1.6 %collective-permute-start.1 = (bf16[4,8,576]{2,0,1:T(4,128)(2,1)S(1)}, bf16[4,8,576]{2,0,1:T(4,128)(2,1)S(1)}, u32[]{:S(2)}, u32[]{:S(2)}) collective-permute-start(bf16[4,8,576]{2,0,1:T(4,128)(2,1)S(1)} %collective-permute-done), channel_id=1, source_target_pairs={{0,2},{2,4},{4,6},{6,8},{8,10},{10,12},{12,14},{14,0},{1,3},{3,5},... | collective-permute-start | bytes 110600 | tf_op jit(solution)/shard_map/ppermute | solution.py:32
  19.3 4.6 %collective-permute-done.1 = bf16[4,8,576]{2,0,1:T(4,128)(2,1)S(1)} collective-permute-done((bf16[4,8,576]{2,0,1:T(4,128)(2,1)S(1)}, bf16[4,8,576]{2,0,1:T(4,128)(2,1)S(1)}, u32[]{:S(2)}, u32[]{:S(2)}) %collective-permute-start.1) | collective-permute-done | bytes 36896 | tf_op jit(solution)/shard_map/ppermute | solution.py:32
  24.5 6.1 %collective-permute-done.2 = bf16[4,8,576]{2,0,1:T(4,128)(2,1)S(1)} collective-permute-done((bf16[4,8,576]{2,0,1:T(4,128)(2,1)S(1)}, bf16[4,8,576]{2,0,1:T(4,128)(2,1)S(1)}, u32[]{:S(2)}, u32[]{:S(2)}) %collective-permute-start.2) | collective-permute-done | bytes 36896 | tf_op jit(solution)/shard_map/ppermute | solution.py:32
  31.2 6.1 %collective-permute-done.3 = bf16[4,8,576]{2,0,1:T(4,128)(2,1)S(1)} collective-permute-done((bf16[4,8,576]{2,0,1:T(4,128)(2,1)S(1)}, bf16[4,8,576]{2,0,1:T(4,128)(2,1)S(1)}, u32[]{:S(2)}, u32[]{:S(2)}) %collective-permute-start.3) | collective-permute-done | bytes 36896 | tf_op jit(solution)/shard_map/ppermute | solution.py:32
  37.9 6.1 %collective-permute-done.4 = bf16[4,8,576]{2,0,1:T(4,128)(2,1)S(1)} collective-permute-done((bf16[4,8,576]{2,0,1:T(4,128)(2,1)S(1)}, bf16[4,8,576]{2,0,1:T(4,128)(2,1)S(1)}, u32[]{:S(2)}, u32[]{:S(2)}) %collective-permute-start.4) | collective-permute-done | bytes 36896 | tf_op jit(solution)/shard_map/ppermute | solution.py:32
  44.6 6.1 %collective-permute-done.5 = bf16[4,8,576]{2,0,1:T(4,128)(2,1)S(1)} collective-permute-done((bf16[4,8,576]{2,0,1:T(4,128)(2,1)S(1)}, bf16[4,8,576]{2,0,1:T(4,128)(2,1)S(1)}, u32[]{:S(2)}, u32[]{:S(2)}) %collective-permute-start.5) | collective-permute-done | bytes 36896 | tf_op jit(solution)/shard_map/ppermute | solution.py:32
  51.3 6.1 %collective-permute-done.6 = bf16[4,8,576]{2,0,1:T(4,128)(2,1)S(1)} collective-permute-done((bf16[4,8,576]{2,0,1:T(4,128)(2,1)S(1)}, bf16[4,8,576]{2,0,1:T(4,128)(2,1)S(1)}, u32[]{:S(2)}, u32[]{:S(2)}) %collective-permute-start.6) | collective-permute-done | bytes 36896 | tf_op jit(solution)/shard_map/ppermute | solution.py:32
  58.0 2.3 %convolution_multiply_fusion = f32[4,64,512]{2,1,0:T(8,128)} fusion(bf16[4,64,576]{2,1,0:T(8,128)(2,1)} %copy_dynamic-update-slice_fusion, bf16[4,512,576]{1,2,0:T(8,128)(2,1)S(1)} %copy-done.1), kind=kOutput, calls=%fused_computation.6 | convolution fusion | flops 151126016 | bytes 3178496 | tf_op jit(solution)/shard_map/rhd,rtd->rht/dot_general | solution.py:72
  60.3 1.2 %reshape.136 = f32[4,64,8,64]{3,2,1,0:T(8,128)S(1)} reshape(f32[4,64,512]{2,1,0:T(8,128)} %convolution_multiply_fusion) | data formatting | bytes 1048576 | tf_op jit(solution)/shard_map/reshape | solution.py:75
  63.3 3.3 %all-to-all-start.2 = ((f32[4,8,8]{2,0,1:T(4,128)}), f32[4,8,8]{2,0,1:T(4,128)S(1)}, u32[]{:S(2)}, u32[]{:S(2)}) async-start(f32[4,8,8]{2,0,1:T(4,128)} %copy.150), calls=%async_computation.2 | async-start | bytes 32768 | tf_op jit(solution)/shard_map/all_to_all | solution.py:100
  66.7 4.3 %convolution_bitcast_fusion = f32[4,64,8,512]{3,1,2,0:T(8,128)} fusion(bf16[4,8,64,576]{3,2,1,0:T(8,128)(2,1)} %bitcast.22, f32[4,64,8,64]{3,2,1,0:T(8,128)S(1)} %reshape.136, f32[4,64,8]{1,2,0:T(8,128)S(1)} %fusion.6, pred[4,8,64]{2,1,0:T(8,128)(4,1)S(1)} %broadcast_compare_fusion), kind=kOutput, calls=%fused_computation.4 | convolution fusion | flops 134742016 | bytes 6825984 | tf_op jit(solution)/shard_map/rhpt,rptl->rhpl/dot_general | solution.py:82
  71.7 1.5 %all-to-all-done.2 = f32[4,8,8]{2,0,1:T(4,128)S(1)} async-done(((f32[4,8,8]{2,0,1:T(4,128)}), f32[4,8,8]{2,0,1:T(4,128)S(1)}, u32[]{:S(2)}, u32[]{:S(2)}) %all-to-all-start.2) | async-done | bytes 1056 | tf_op jit(solution)/shard_map/all_to_all | solution.py:100
  73.2 4.5 %all-to-all-start = ((f32[4,8,8]{2,0,1:T(4,128)}), f32[4,8,8]{2,0,1:T(4,128)S(1)}, u32[]{:S(2)}, u32[]{:S(2)}) async-start(f32[4,8,8]{2,0,1:T(4,128)} %copy.147), calls=%async_computation | async-start | bytes 32768 | tf_op jit(solution)/shard_map/all_to_all | solution.py:93
  77.7 8.2 %fusion = f32[4,64,1,512]{3,2,1,0:T(1,128)S(1)} fusion(f32[4,64,8,1]{2,3,1,0:T(1,128)S(1)} %copy.154, f32[4,64,8,512]{3,1,2,0:T(8,128)} %convolution_bitcast_fusion), kind=kOutput, calls=%fused_computation | convolution fusion | flops 12582912 | bytes 4726784 | tf_op jit(solution)/shard_map/rhp,rhpl->rhl/dot_general | solution.py:91
  86.0 0.8 copy.149
  86.8 6.0 %all-to-all-start.1 = ((f32[4,8,8,512]{3,2,0,1:T(8,128)}), f32[4,8,8,512]{3,2,0,1:T(8,128)S(1)}, u32[]{:S(2)}, u32[]{:S(2)}) async-start(f32[4,8,8,512]{3,2,0,1:T(8,128)} %copy.149), calls=%async_computation.1 | async-start | bytes 1048576 | tf_op jit(solution)/shard_map/all_to_all | solution.py:107
  92.8 1.8 %fusion.7 = f32[4,64,8]{1,2,0:T(8,128)S(1)} fusion(bf16[4,64,576]{2,1,0:T(8,128)(2,1)} %copy_dynamic-update-slice_fusion, bf16[4,8,576]{2,1,0:T(8,128)(2,1)S(1)} %copy-done.3, bf16[4,8,576]{2,1,0:T(8,128)(2,1)S(1)} %get-tuple-element.18, pred[4,8]{1,0:T(4,128)(4,1)S(1)} %slice_reduce_fusion), kind=kOutput, calls=%fused_computation.17 | convolution fusion | flops 14561280 | bytes 376864 | tf_op jit(solution)/shard_map/rhd,rpd->rhp/dot_general | solution.py:62
  94.6 1.5 %fusion.4 = f32[4,64,8]{1,2,0:T(8,128)S(1)} fusion(f32[4,64,8]{1,2,0:T(8,128)S(1)} %fusion.7, bf16[4,64,576]{2,1,0:T(8,128)(2,1)} %copy_dynamic-update-slice_fusion, bf16[4,8,576]{2,1,0:T(8,128)(2,1)S(1)} %copy-done.3, bf16[4,8,576]{2,1,0:T(8,128)(2,1)S(1)} %get-tuple-element.18, pred[4,8]{1,0:T(4,128)(4,1)S(1)} %slice_reduce_fusion), kind=kOutput, calls=%fused_computation.10 | convolution fusion | flops 14270464 | bytes 385056 | tf_op jit(solution)/shard_map/rhd,rpd->rhp/dot_general | solution.py:61
  96.2 3.4 %pmax.7 = f32[4,8,8]{2,1,0:T(8,128)S(1)} all-reduce(f32[4,8,8]{2,1,0:T(8,128)S(1)} %select_reduce_fusion.2), channel_id=1, replica_groups=mesh['grp'=2,'seq'=8,'head'=2] {'head'}, use_global_device_ids=true, to_apply=%region_12.13 | all-reduce | flops 256 | bytes 2048 | tf_op jit(solution)/shard_map/pmax | solution.py:67
  100.2 2.9 %all-to-all-done.1 = f32[4,8,8,512]{3,2,0,1:T(8,128)S(1)} async-done(((f32[4,8,8,512]{3,2,0,1:T(8,128)}), f32[4,8,8,512]{3,2,0,1:T(8,128)S(1)}, u32[]{:S(2)}, u32[]{:S(2)}) %all-to-all-start.1) | async-done | bytes 524320 | tf_op jit(solution)/shard_map/all_to_all | solution.py:107
  (61 shorter events, 13.6 us)
Async XLA Ops:
  0.6 1.2 %copy-start = (bf16[8,128,512]{2,1,0:T(8,128)(2,1)S(1)}, bf16[8,128,512]{2,1,0:T(8,128)(2,1)}, u32[]{:S(2)}) copy-start(bf16[8,128,512]{2,1,0:T(8,128)(2,1)} %param.9) | copy-start | bytes 3145732
  2.9 14.3 %collective-permute-start = (bf16[4,8,576]{2,0,1:T(4,128)(2,1)S(1)}, bf16[4,8,576]{2,0,1:T(4,128)(2,1)S(1)}, u32[]{:S(2)}, u32[]{:S(2)}) collective-permute-start(bf16[4,8,576]{2,0,1:T(4,128)(2,1)S(1)} %pad_maximum_fusion), channel_id=1, source_target_pairs={{0,2},{2,4},{4,6},{6,8},{8,10},{10,12},{12,14},{14,0},{1,3},{3,5},... | collective-permute-start | bytes 110600 | tf_op jit(solution)/shard_map/ppermute | solution.py:32
  7.0 5.8 %copy-start.6 = (s32[4]{0:T(128)S(1)}, s32[4]{0:T(128)}, u32[]{:S(2)}) copy-start(s32[4]{0:T(128)} %param.12) | copy-start | bytes 52
  11.4 4.6 %copy-start.4 = (s32[4,8,32]{2,1,0:T(8,128)S(1)}, s32[4,8,32]{2,1,0:T(8,128)}, u32[]{:S(2)}) copy-start(s32[4,8,32]{2,1,0:T(8,128)} %param.13) | copy-start | bytes 12292
  11.4 46.6 %copy-start.1 = (bf16[4,512,576]{1,2,0:T(8,128)(2,1)S(1)}, bf16[4,512,576]{1,2,0:T(8,128)(2,1)}, u32[]{:S(2)}) copy-start(bf16[4,512,576]{1,2,0:T(8,128)(2,1)} %param.11) | copy-start | bytes 7077892
  11.4 4.6 %copy-start.7 = (s32[8]{0:T(128)S(1)}, s32[8]{0:T(128)}, u32[]{:S(2)}) copy-start(s32[8]{0:T(128)} %iota_add_fusion) | copy-start | bytes 100
  11.4 5.3 %copy-start.5 = (pred[64,8]{0,1:T(8,128)(4,1)S(1)}, pred[64,8]{0,1:T(8,128)(4,1)}, u32[]{:S(2)}) copy-start(pred[64,8]{0,1:T(8,128)(4,1)} %iota_compare_fusion.1) | copy-start | bytes 1540
  17.1 6.8 %collective-permute-start.1 = (bf16[4,8,576]{2,0,1:T(4,128)(2,1)S(1)}, bf16[4,8,576]{2,0,1:T(4,128)(2,1)S(1)}, u32[]{:S(2)}, u32[]{:S(2)}) collective-permute-start(bf16[4,8,576]{2,0,1:T(4,128)(2,1)S(1)} %collective-permute-done), channel_id=1, source_target_pairs={{0,2},{2,4},{4,6},{6,8},{8,10},{10,12},{12,14},{14,0},{1,3},{3,5},... | collective-permute-start | bytes 110600 | tf_op jit(solution)/shard_map/ppermute | solution.py:32
  23.9 6.7 %collective-permute-start.2 = (bf16[4,8,576]{2,0,1:T(4,128)(2,1)S(1)}, bf16[4,8,576]{2,0,1:T(4,128)(2,1)S(1)}, u32[]{:S(2)}, u32[]{:S(2)}) collective-permute-start(bf16[4,8,576]{2,0,1:T(4,128)(2,1)S(1)} %collective-permute-done.1), channel_id=1, source_target_pairs={{0,2},{2,4},{4,6},{6,8},{8,10},{10,12},{12,14},{14,0},{1,3},{3,5},... | collective-permute-start | bytes 110600 | tf_op jit(solution)/shard_map/ppermute | solution.py:32
  30.6 6.7 %collective-permute-start.3 = (bf16[4,8,576]{2,0,1:T(4,128)(2,1)S(1)}, bf16[4,8,576]{2,0,1:T(4,128)(2,1)S(1)}, u32[]{:S(2)}, u32[]{:S(2)}) collective-permute-start(bf16[4,8,576]{2,0,1:T(4,128)(2,1)S(1)} %collective-permute-done.2), channel_id=1, source_target_pairs={{0,2},{2,4},{4,6},{6,8},{8,10},{10,12},{12,14},{14,0},{1,3},{3,5},... | collective-permute-start | bytes 110600 | tf_op jit(solution)/shard_map/ppermute | solution.py:32
  37.3 6.7 %collective-permute-start.4 = (bf16[4,8,576]{2,0,1:T(4,128)(2,1)S(1)}, bf16[4,8,576]{2,0,1:T(4,128)(2,1)S(1)}, u32[]{:S(2)}, u32[]{:S(2)}) collective-permute-start(bf16[4,8,576]{2,0,1:T(4,128)(2,1)S(1)} %collective-permute-done.3), channel_id=1, source_target_pairs={{0,2},{2,4},{4,6},{6,8},{8,10},{10,12},{12,14},{14,0},{1,3},{3,5},... | collective-permute-start | bytes 110600 | tf_op jit(solution)/shard_map/ppermute | solution.py:32
  44.0 6.7 %collective-permute-start.5 = (bf16[4,8,576]{2,0,1:T(4,128)(2,1)S(1)}, bf16[4,8,576]{2,0,1:T(4,128)(2,1)S(1)}, u32[]{:S(2)}, u32[]{:S(2)}) collective-permute-start(bf16[4,8,576]{2,0,1:T(4,128)(2,1)S(1)} %collective-permute-done.4), channel_id=1, source_target_pairs={{0,2},{2,4},{4,6},{6,8},{8,10},{10,12},{12,14},{14,0},{1,3},{3,5},... | collective-permute-start | bytes 110600 | tf_op jit(solution)/shard_map/ppermute | solution.py:32
  50.7 6.7 %collective-permute-start.6 = (bf16[4,8,576]{2,0,1:T(4,128)(2,1)S(1)}, bf16[4,8,576]{2,0,1:T(4,128)(2,1)S(1)}, u32[]{:S(2)}, u32[]{:S(2)}) collective-permute-start(bf16[4,8,576]{2,0,1:T(4,128)(2,1)S(1)} %collective-permute-done.5), channel_id=1, source_target_pairs={{0,2},{2,4},{4,6},{6,8},{8,10},{10,12},{12,14},{14,0},{1,3},{3,5},... | collective-permute-start | bytes 110600 | tf_op jit(solution)/shard_map/ppermute | solution.py:32
  63.3 9.9 %all-to-all-start.2 = ((f32[4,8,8]{2,0,1:T(4,128)}), f32[4,8,8]{2,0,1:T(4,128)S(1)}, u32[]{:S(2)}, u32[]{:S(2)}) async-start(f32[4,8,8]{2,0,1:T(4,128)} %copy.150), calls=%async_computation.2 | async-start | bytes 32768 | tf_op jit(solution)/shard_map/all_to_all | solution.py:100
  73.2 13.6 %all-to-all-start = ((f32[4,8,8]{2,0,1:T(4,128)}), f32[4,8,8]{2,0,1:T(4,128)S(1)}, u32[]{:S(2)}, u32[]{:S(2)}) async-start(f32[4,8,8]{2,0,1:T(4,128)} %copy.147), calls=%async_computation | async-start | bytes 32768 | tf_op jit(solution)/shard_map/all_to_all | solution.py:93
  85.9 6.9 %copy-start.3 = (bf16[4,8,576]{2,1,0:T(8,128)(2,1)S(1)}, bf16[4,8,576]{2,1,0:T(8,128)(2,1)}, u32[]{:S(2)}) copy-start(bf16[4,8,576]{2,1,0:T(8,128)(2,1)} %get-tuple-element.19) | copy-start | bytes 110596
  85.9 17.4 %copy-start.2 = (bf16[8,512,128]{2,1,0:T(8,128)(2,1)S(1)}, bf16[8,512,128]{2,1,0:T(8,128)(2,1)}, u32[]{:S(2)}) copy-start(bf16[8,512,128]{2,1,0:T(8,128)(2,1)} %param.10) | copy-start | bytes 3145732
  86.8 16.3 %all-to-all-start.1 = ((f32[4,8,8,512]{3,2,0,1:T(8,128)}), f32[4,8,8,512]{3,2,0,1:T(8,128)S(1)}, u32[]{:S(2)}, u32[]{:S(2)}) async-start(f32[4,8,8,512]{3,2,0,1:T(8,128)} %copy.149), calls=%async_computation.1 | async-start | bytes 1048576 | tf_op jit(solution)/shard_map/all_to_all | solution.py:107
